TPU v7x, 32 devices: a whole 2x2x4 slice. The times are simulated.
32 devices in a mesh: pair: 8 (over y, x, core), aux: 4 (over z).
Axes of the slice: x: 2, y: 2, z: 4, core: 2. Of those that a mesh axis runs over, the one named last changes fastest.
Arguments:
- three_center: float32 [2048, 8192], P('aux', 'pair'), may hold values from -0.0625 to 0.0625
- densities: float32 [8192, 512], P(('pair', 'aux')), may hold values from -6 to 6
- screen_mask: int32 [32, 128], P('aux', 'pair'), may hold values 0 or 1
- diag_inverse: float32 [2048, 512], P('aux'), as said below
- sub_factor: float32 [2048, 512], P('aux'), as said below
Outputs:
- response: float32 [8192, 512], P(('pair', 'aux'))
Inputs may be any that keep to these rules, and one draw needn't show every extreme that they name: `diag_inverse`: each block of 512 rows is lower triangular; its diagonal lies in 0.75 to 1.3 and its entries below the diagonal within plus or minus 2 / sqrt(512). `sub_factor`: block 0 is not used; entries lie within plus or minus 3.4 / sqrt(512).
All inputs are finite; a program needn't handle non-finite values. No bound on the sum of `screen_mask` on one device may be relied on, other than what follows from the above.
Results may differ from a plain program's by a relative error of at most 0.0003.
Values sent between devices are 32-bit elements; how exact they have to be, the bound alone decides.
No kernel may reach another device: no remote copies, remote signals or barrier semaphores. Data moves between devices by JAX's collectives and lax.ppermute only.
A program may use at most 192 MiB of HBM per device.

v0:
```python
import jax
import jax.numpy as jnp
from jax import lax
from jax.sharding import PartitionSpec as P


def from_behind(array, axis, by):
    count = lax.axis_size(axis)
    pairs = [(i, i + by) for i in range(count) if 0 <= i + by < count]
    return lax.ppermute(array, axis, pairs)


def screen_block(block, screen_mask):
    aux_blocks, pair_blocks = screen_mask.shape
    aux_size = block.shape[0] // aux_blocks
    pair_size = block.shape[1] // pair_blocks
    shaped = block.reshape(aux_blocks, aux_size, pair_blocks, pair_size)
    shaped = shaped * screen_mask.astype(jnp.float32)[:, None, :, None]
    return shaped.reshape(block.shape)


def product(left, right):
    return jnp.dot(left, right, precision=lax.Precision.HIGHEST, preferred_element_type=jnp.float32)


def contract_first(left, right):
    return lax.dot_general(
        left,
        right,
        (((0,), (0,)), ((), ())),
        precision=lax.Precision.HIGHEST,
        preferred_element_type=jnp.float32,
    )


def per_device(three_center, densities, screen_mask, diag_inverse, sub_factor):
    screened = screen_block(three_center, screen_mask)
    dens_full = lax.all_gather(densities, "aux", axis=0, tiled=True)
    gamma_share = lax.psum_scatter(
        contract_first(dens_full, screened.T), "pair", scatter_dimension=0, tiled=True
    )
    right_side = gamma_share.T
    transfer = -product(diag_inverse, sub_factor)
    driving = product(diag_inverse, right_side)
    chain_length = lax.axis_size("aux")

    def forward(turn_index, incoming):
        return from_behind(product(transfer, incoming) + driving, "aux", 1)

    incoming = lax.fori_loop(0, chain_length - 1, forward, jnp.zeros_like(driving))
    solved = product(transfer, incoming) + driving
    source = product(sub_factor.T, product(diag_inverse.T, solved))
    back_map = transfer.T

    def backward(turn_index, arriving):
        return from_behind(product(back_map, arriving) + source, "aux", -1)

    arriving = lax.fori_loop(0, chain_length - 1, backward, jnp.zeros_like(driving))
    coefficients = product(diag_inverse.T, solved - arriving)
    coeff_full = lax.all_gather(coefficients, "pair", axis=1, tiled=True)
    return lax.psum_scatter(
        contract_first(screened, coeff_full), "aux", scatter_dimension=0, tiled=True
    )


def solution(mesh):
    return jax.shard_map(
        per_device,
        mesh=mesh,
        in_specs=(
            P("aux", "pair"),
            P(("pair", "aux"), None),
            P("aux", "pair"),
            P("aux", None),
            P("aux", None),
        ),
        out_specs=P(("pair", "aux"), None),
        check_vma=False,
    )
```

profile of v0, /device:TPU:0, one launch (start us, length us, event | category | flops | bytes accessed | tf_op | source)
XLA Modules:
  0.0 238.7 jit_solution(8295645147686337585)
XLA Ops:
  6.5 0.0 copy-start
  6.5 0.0 all-gather.3.cloned.1.call-start
  6.5 0.7 all-gather.3.cloned.1.call-update
  7.3 0.0 reduce-scatter.7.cloned.1.call-start
  7.3 0.7 convert_element_type.3
  8.0 2.3 mul.11
  10.3 4.9 %mul.12 = f32[512,1024]{1,0:T(8,128)} reshape(f32[8,64,16,64]{3,2,1,0:T(8,128)} %mul.11) | data formatting | bytes 4194304 | tf_op jit(solution)/shard_map/mul | solution.py:18
  15.2 2.6 %mul.13 = f32[512,1024]{1,0:T(8,128)S(1)} multiply(f32[512,1024]{1,0:T(8,128)} %param.9, f32[512,1024]{1,0:T(8,128)} %mul.12) | non-fusion elementwise | flops 524288 | bytes 6291456 | tf_op jit(solution)/shard_map/mul | solution.py:18
  17.8 0.0 copy-start.1
  17.8 39.8 %all-gather.3.cloned.1.call-done = f32[1024,512]{1,0:T(8,128)} async-done(((f32[256,512]{1,0:T(8,128)}), f32[1024,512]{1,0:T(8,128)}) %all-gather.3.cloned.1.call-update) | async-done | bytes 2097168 | tf_op jit(solution)/shard_map/all_gather | solution.py:38
  57.6 6.1 %convolution_bitcast_fusion = f32[512,512]{0,1:T(8,128)} fusion(f32[512,1024]{1,0:T(8,128)S(1)} %mul.13, f32[1024,512]{1,0:T(8,128)} %all-gather.3.cloned.1.call-done), kind=kOutput, calls=%fused_computation.2 | convolution fusion | flops 3221225472 | bytes 5242880 | tf_op jit(solution)/shard_map/dot_general | solution.py:27
  63.7 2.5 %copy.8 = f32[512,512]{1,0:T(8,128)} copy(f32[512,512]{0,1:T(8,128)} %convolution_bitcast_fusion) | data formatting | bytes 2097152
  66.2 0.0 reduce-scatter.7.cloned.1.call-update
  66.3 0.2 all-gather.5.cloned.1.call-start
  66.5 3.1 %convolution_negate_fusion = f32[512,512]{1,0:T(8,128)S(1)} fusion(f32[512,512]{1,0:T(8,128)S(1)} %copy-done, f32[512,512]{1,0:T(8,128)} %param.13), kind=kOutput, calls=%fused_computation.3 | convolution fusion | flops 1610874880 | bytes 3145728 | tf_op jit(solution)/shard_map/dot_general | solution.py:23
  69.6 0.3 copy.7
  69.9 31.3 %reduce-scatter.7.cloned.1.call-done = f32[64,512]{1,0:T(8,128)} async-done(((f32[512,512]{1,0:T(8,128)}), f32[64,512]{1,0:T(8,128)}) %reduce-scatter.7.cloned.1.call-update) | async-done | bytes 131088
  101.2 2.0 convolution_bitcast_fusion.3
  103.2 23.2 %while.20 = (s32[]{:T(128)}, f32[512,64]{0,1:T(8,128)S(1)}, f32[512,512]{1,0:T(8,128)S(1)}, f32[512,64]{0,1:T(8,128)S(1)}, s32[]{:T(128)}) while((s32[]{:T(128)}, f32[512,64]{0,1:T(8,128)S(1)}, f32[512,512]{1,0:T(8,128)S(1)}, f32[512,64]{0,1:T(8,128)S(1)}, s32[]{:T(128)}) %tuple.33), condition=%wide.region_2.0_spmd, body=%wide.region_1.0_spmd.sunk | while | flops 201359360 | bytes 1966181 | solution.py:50
  103.2 1.1 convolution_add_fusion.5
  104.4 3.4 %collective-permute-start = (f32[512,64]{0,1:T(8,128)S(1)}, f32[512,64]{0,1:T(8,128)S(1)}, u32[]{:S(2)}, u32[]{:S(2)}) collective-permute-start(f32[512,64]{0,1:T(8,128)S(1)} %convolution_add_fusion.5), channel_id=1, source_target_pairs={{0,1},{1,2},{2,3},{4,5},{5,6},{6,7},{8,9},{9,10},{10,11},{12,13},{... | collective-permute-start | bytes 393224 | tf_op jit(solution)/shard_map/while/body/eval_jaxpr/ppermute | solution.py:10
  107.8 2.6 %collective-permute-done = f32[512,64]{0,1:T(8,128)S(1)} collective-permute-done((f32[512,64]{0,1:T(8,128)S(1)}, f32[512,64]{0,1:T(8,128)S(1)}, u32[]{:S(2)}, u32[]{:S(2)}) %collective-permute-start) | collective-permute-done | bytes 131104 | tf_op jit(solution)/shard_map/while/body/eval_jaxpr/ppermute | solution.py:10
  110.4 1.1 convolution_add_fusion.5
  111.5 4.4 %collective-permute-start = (f32[512,64]{0,1:T(8,128)S(1)}, f32[512,64]{0,1:T(8,128)S(1)}, u32[]{:S(2)}, u32[]{:S(2)}) collective-permute-start(f32[512,64]{0,1:T(8,128)S(1)} %convolution_add_fusion.5), channel_id=1, source_target_pairs={{0,1},{1,2},{2,3},{4,5},{5,6},{6,7},{8,9},{9,10},{10,11},{12,13},{... | collective-permute-start | bytes 393224 | tf_op jit(solution)/shard_map/while/body/eval_jaxpr/ppermute | solution.py:10
  115.9 2.5 %collective-permute-done = f32[512,64]{0,1:T(8,128)S(1)} collective-permute-done((f32[512,64]{0,1:T(8,128)S(1)}, f32[512,64]{0,1:T(8,128)S(1)}, u32[]{:S(2)}, u32[]{:S(2)}) %collective-permute-start) | collective-permute-done | bytes 131104 | tf_op jit(solution)/shard_map/while/body/eval_jaxpr/ppermute | solution.py:10
  118.4 1.1 convolution_add_fusion.5
  119.5 4.4 %collective-permute-start = (f32[512,64]{0,1:T(8,128)S(1)}, f32[512,64]{0,1:T(8,128)S(1)}, u32[]{:S(2)}, u32[]{:S(2)}) collective-permute-start(f32[512,64]{0,1:T(8,128)S(1)} %convolution_add_fusion.5), channel_id=1, source_target_pairs={{0,1},{1,2},{2,3},{4,5},{5,6},{6,7},{8,9},{9,10},{10,11},{12,13},{... | collective-permute-start | bytes 393224 | tf_op jit(solution)/shard_map/while/body/eval_jaxpr/ppermute | solution.py:10
  123.9 2.5 %collective-permute-done = f32[512,64]{0,1:T(8,128)S(1)} collective-permute-done((f32[512,64]{0,1:T(8,128)S(1)}, f32[512,64]{0,1:T(8,128)S(1)}, u32[]{:S(2)}, u32[]{:S(2)}) %collective-permute-start) | collective-permute-done | bytes 131104 | tf_op jit(solution)/shard_map/while/body/eval_jaxpr/ppermute | solution.py:10
  126.4 1.1 convolution_add_fusion.2
  127.5 0.8 fusion.1
  128.3 0.8 convolution_bitcast_fusion.2
  129.1 24.6 %while.21 = (s32[]{:T(128)}, f32[512,64]{0,1:T(8,128)S(1)}, f32[512,512]{1,0:T(8,128)S(1)}, f32[512,64]{0,1:T(8,128)S(1)}, s32[]{:T(128)}) while((s32[]{:T(128)}, f32[512,64]{0,1:T(8,128)S(1)}, f32[512,512]{1,0:T(8,128)S(1)}, f32[512,64]{0,1:T(8,128)S(1)}, s32[]{:T(128)}) %tuple.36), condition=%wide.region_4.0_spmd, body=%wide.region_3.0_spmd.sunk | while | flops 201359360 | bytes 1966181 | solution.py:58
  129.1 1.1 convolution_add_fusion.6
  130.2 1.3 collective-permute-start.1
  131.5 6.0 %collective-permute-done.1 = f32[512,64]{0,1:T(8,128)S(1)} collective-permute-done((f32[512,64]{0,1:T(8,128)S(1)}, f32[512,64]{0,1:T(8,128)S(1)}, u32[]{:S(2)}, u32[]{:S(2)}) %collective-permute-start.1) | collective-permute-done | bytes 131104 | tf_op jit(solution)/shard_map/while/body/eval_jaxpr/ppermute | solution.py:10
  137.5 1.1 convolution_add_fusion.6
  138.7 1.3 collective-permute-start.1
  140.0 5.6 %collective-permute-done.1 = f32[512,64]{0,1:T(8,128)S(1)} collective-permute-done((f32[512,64]{0,1:T(8,128)S(1)}, f32[512,64]{0,1:T(8,128)S(1)}, u32[]{:S(2)}, u32[]{:S(2)}) %collective-permute-start.1) | collective-permute-done | bytes 131104 | tf_op jit(solution)/shard_map/while/body/eval_jaxpr/ppermute | solution.py:10
  145.5 1.1 convolution_add_fusion.6
  146.7 1.3 collective-permute-start.1
  148.0 5.7 %collective-permute-done.1 = f32[512,64]{0,1:T(8,128)S(1)} collective-permute-done((f32[512,64]{0,1:T(8,128)S(1)}, f32[512,64]{0,1:T(8,128)S(1)}, u32[]{:S(2)}, u32[]{:S(2)}) %collective-permute-start.1) | collective-permute-done | bytes 131104 | tf_op jit(solution)/shard_map/while/body/eval_jaxpr/ppermute | solution.py:10
  153.6 1.4 convolution_bitcast_fusion.1
  155.1 0.0 all-gather.5.cloned.1.call-update
  155.1 0.3 reduce-scatter.5.cloned.1.call-start
  155.3 23.0 %all-gather.5.cloned.1.call-done = f32[512,512]{0,1:T(8,128)} async-done(((f32[512,64]{0,1:T(8,128)}), f32[512,512]{0,1:T(8,128)}) %all-gather.5.cloned.1.call-update) | async-done | bytes 1048592 | tf_op jit(solution)/shard_map/all_gather | solution.py:60
  178.3 9.8 %fusion.2 = f32[1024,512]{1,0:T(8,128)} fusion(f32[512,1024]{1,0:T(8,128)} %copy-done.1, f32[512,512]{0,1:T(8,128)} %all-gather.5.cloned.1.call-done), kind=kOutput, calls=%fused_computation.10 | convolution fusion | flops 3221225472 | bytes 5242880 | tf_op jit(solution)/shard_map/dot_general | solution.py:27
  188.1 0.0 reduce-scatter.5.cloned.1.call-update
  188.2 44.0 %reduce-scatter.5.cloned.1.call-done = f32[256,512]{1,0:T(8,128)} async-done(((f32[1024,512]{1,0:T(8,128)}), f32[256,512]{1,0:T(8,128)}) %reduce-scatter.5.cloned.1.call-update) | async-done | bytes 524304 | tf_op jit(solution)/shard_map/reduce_scatter | solution.py:61
  (6 shorter events, 0.0 us)
Async XLA Ops:
  6.5 59.9 %copy-start = (f32[512,512]{1,0:T(8,128)S(1)}, f32[512,512]{1,0:T(8,128)}, u32[]{:S(2)}) copy-start(f32[512,512]{1,0:T(8,128)} %param.12) | copy-start | bytes 3145732
  6.5 51.1 %all-gather.3.cloned.1.call-start = ((), (), s32[]{:S(2)}) async-start(), calls=%async_computation.2 | async-start | bytes 2621440 | tf_op jit(solution)/shard_map/all_gather | solution.py:38
  7.3 93.9 %reduce-scatter.7.cloned.1.call-start = ((), (), s32[]{:S(2)}) async-start(), calls=%async_computation.5 | async-start | bytes 1179648
  17.8 45.9 %copy-start.1 = (f32[512,1024]{1,0:T(8,128)}, f32[512,1024]{1,0:T(8,128)S(1)}, u32[]{:S(2)}) copy-start(f32[512,1024]{1,0:T(8,128)S(1)} %mul.13) | copy-start | bytes 6291460
  66.3 112.1 %all-gather.5.cloned.1.call-start = ((), (), s32[]{:S(2)}) async-start(), calls=%async_computation.3 | async-start | bytes 1179648 | tf_op jit(solution)/shard_map/all_gather | solution.py:60
  104.4 6.0 %collective-permute-start = (f32[512,64]{0,1:T(8,128)S(1)}, f32[512,64]{0,1:T(8,128)S(1)}, u32[]{:S(2)}, u32[]{:S(2)}) collective-permute-start(f32[512,64]{0,1:T(8,128)S(1)} %convolution_add_fusion.5), channel_id=1, source_target_pairs={{0,1},{1,2},{2,3},{4,5},{5,6},{6,7},{8,9},{9,10},{10,11},{12,13},{... | collective-permute-start | bytes 393224 | tf_op jit(solution)/shard_map/while/body/eval_jaxpr/ppermute | solution.py:10
  111.5 6.9 %collective-permute-start = (f32[512,64]{0,1:T(8,128)S(1)}, f32[512,64]{0,1:T(8,128)S(1)}, u32[]{:S(2)}, u32[]{:S(2)}) collective-permute-start(f32[512,64]{0,1:T(8,128)S(1)} %convolution_add_fusion.5), channel_id=1, source_target_pairs={{0,1},{1,2},{2,3},{4,5},{5,6},{6,7},{8,9},{9,10},{10,11},{12,13},{... | collective-permute-start | bytes 393224 | tf_op jit(solution)/shard_map/while/body/eval_jaxpr/ppermute | solution.py:10
  119.5 6.9 %collective-permute-start = (f32[512,64]{0,1:T(8,128)S(1)}, f32[512,64]{0,1:T(8,128)S(1)}, u32[]{:S(2)}, u32[]{:S(2)}) collective-permute-start(f32[512,64]{0,1:T(8,128)S(1)} %convolution_add_fusion.5), channel_id=1, source_target_pairs={{0,1},{1,2},{2,3},{4,5},{5,6},{6,7},{8,9},{9,10},{10,11},{12,13},{... | collective-permute-start | bytes 393224 | tf_op jit(solution)/shard_map/while/body/eval_jaxpr/ppermute | solution.py:10
  126.4 1.9 copy-start.2
  130.2 7.3 %collective-permute-start.1 = (f32[512,64]{0,1:T(8,128)S(1)}, f32[512,64]{0,1:T(8,128)S(1)}, u32[]{:S(2)}, u32[]{:S(2)}) collective-permute-start(f32[512,64]{0,1:T(8,128)S(1)} %convolution_add_fusion.6), channel_id=1, source_target_pairs={{1,0},{2,1},{3,2},{5,4},{6,5},{7,6},{9,8},{10,9},{11,10},{13,12},{... | collective-permute-start | bytes 393224 | tf_op jit(solution)/shard_map/while/body/eval_jaxpr/ppermute | solution.py:10
  138.7 6.9 %collective-permute-start.1 = (f32[512,64]{0,1:T(8,128)S(1)}, f32[512,64]{0,1:T(8,128)S(1)}, u32[]{:S(2)}, u32[]{:S(2)}) collective-permute-start(f32[512,64]{0,1:T(8,128)S(1)} %convolution_add_fusion.6), channel_id=1, source_target_pairs={{1,0},{2,1},{3,2},{5,4},{6,5},{7,6},{9,8},{10,9},{11,10},{13,12},{... | collective-permute-start | bytes 393224 | tf_op jit(solution)/shard_map/while/body/eval_jaxpr/ppermute | solution.py:10
  146.7 7.0 %collective-permute-start.1 = (f32[512,64]{0,1:T(8,128)S(1)}, f32[512,64]{0,1:T(8,128)S(1)}, u32[]{:S(2)}, u32[]{:S(2)}) collective-permute-start(f32[512,64]{0,1:T(8,128)S(1)} %convolution_add_fusion.6), channel_id=1, source_target_pairs={{1,0},{2,1},{3,2},{5,4},{6,5},{7,6},{9,8},{10,9},{11,10},{13,12},{... | collective-permute-start | bytes 393224 | tf_op jit(solution)/shard_map/while/body/eval_jaxpr/ppermute | solution.py:10
  155.1 77.1 %reduce-scatter.5.cloned.1.call-start = ((), (), s32[]{:S(2)}) async-start(), calls=%async_computation.4 | async-start | bytes 2621440 | tf_op jit(solution)/shard_map/reduce_scatter | solution.py:61
Sparse Core Ops, SparseCore 0:
  8.9 48.6 all-gather.2
  66.4 34.7 reduce-scatter.6
  155.2 23.0 all-gather.4
  188.3 43.8 reduce-scatter.4
where the time goes:
time: 239 us
  waiting for transfers between devices  164 us (69%)
  matrix products  31.9 us (13%)
  starting transfers between devices  16.5 us (7%)
  between operations  13.2 us (6%)
  local copies, waits for them, and re-layouts  10.1 us (4%)
  other arithmetic  3.3 us (1%)
    reduce_scatter x1, waiting for transfers between devices, per_device(): lax.psum_scatter(contract_first(screened, coeff_full), 'aux', scatter_dim...  44 us
    all_gather x1, waiting for transfers between devices, per_device(): dens_full = lax.all_gather(densities, 'aux', axis=0, tiled=True)  39.8 us
    unnamed x5, waiting for transfers between devices  32 us
    ppermute x6, waiting for transfers between devices, from_behind(): return lax.ppermute(array, axis, pairs)  24.8 us
    all_gather x1, waiting for transfers between devices, per_device(): coeff_full = lax.all_gather(coefficients, 'pair', axis=1, tiled=True)  23 us
    ppermute x6, starting transfers between devices, from_behind(): return lax.ppermute(array, axis, pairs)  16 us
    dot_general x12, matrix products, product(): jnp.dot(left, right, precision=lax.Precision.HIGHEST, preferred_element_t...  16 us
    dot_general x2, matrix products, contract_first(): lax.dot_general(left, right, (((0,), (0,)), ((), ())), precision=lax.Prec...  15.9 us
  transfers between devices with their start and end apart: 10, of which 10 were waited for; matrix products, arithmetic and copies ran while one was open for 6% of the time, Pallas kernels for 0%

commit v1 on v0

--- a/solution.py
+++ b/solution.py
@@ -2,6 +2,24 @@
 import jax.numpy as jnp
 from jax import lax
 from jax.sharding import PartitionSpec as P
+
+
+def collect(array, axis, dim):
+    ways, here, step = (lax.axis_size(axis), lax.axis_index(axis), array.shape[dim])
+    dims = [n * ways if d == dim else n for d, n in enumerate(array.shape)]
+    full = lax.dynamic_update_slice_in_dim(
+        jnp.zeros(dims, array.dtype), array, here * step, axis=dim
+    )
+    going_up = going_down = array
+    for far in range(1, ways // 2 + 1):
+        going_up = lax.ppermute(going_up, axis, [(d, (d + 1) % ways) for d in range(ways)])
+        full = lax.dynamic_update_slice_in_dim(full, going_up, (here - far) % ways * step, axis=dim)
+        if 2 * far < ways:
+            going_down = lax.ppermute(going_down, axis, [(d, (d - 1) % ways) for d in range(ways)])
+            full = lax.dynamic_update_slice_in_dim(
+                full, going_down, (here + far) % ways * step, axis=dim
+            )
+    return full
 
 
 def from_behind(array, axis, by):
@@ -57,7 +75,7 @@
 
     arriving = lax.fori_loop(0, chain_length - 1, backward, jnp.zeros_like(driving))
     coefficients = product(diag_inverse.T, solved - arriving)
-    coeff_full = lax.all_gather(coefficients, "pair", axis=1, tiled=True)
+    coeff_full = collect(coefficients, "pair", 1)
     return lax.psum_scatter(
         contract_first(screened, coeff_full), "aux", scatter_dimension=0, tiled=True
     )

time: 239 us -> 240 us (level)
  waiting for transfers between devices: 164 us -> 152 us
  starting transfers between devices: 16.5 us -> 24.2 us
  local copies, waits for them, and re-layouts: 10.1 us -> 15.8 us
    all_gather x1 -> x0, waiting for transfers between devices: 23 us -> none  [per_device(): coeff_full = lax.all_gather(coefficients, 'pair', axis=1, tiled=True)]
    ppermute x0 -> x7, waiting for transfers between devices: none -> 12 us  [the longest x4 12 us: collect(): lax.ppermute(going_up, axis, [(d, (d + 1) % ways) for d in range(ways)])]
    ppermute x0 -> x7, starting transfers between devices: none -> 7.94 us  [the longest x3 7.93 us: collect(): lax.ppermute(going_down, axis, [(d, (d - 1) % ways) for d in range(ways)])]
    dynamic_update_slice x0 -> x7, local copies, waits for them, and re-layouts: none -> 4.64 us  [the longest x4 2.66 us: collect(): lax.dynamic_update_slice_in_dim(full, going_up, (here - far) % ways * ste...]
    unnamed x5 -> x4, waiting for transfers between devices: 32 us -> 32 us
  transfers between devices with their start and end apart: 10 -> 16, of which waited for: 10 -> 13; matrix products, arithmetic and copies ran while one was open for 6% -> 8% of each run, Pallas kernels for 0% -> 0%
where the time goes in v1:
time: 240 us; the launch traced here: 239 us
  waiting for transfers between devices  152 us (63%)
  matrix products  30.6 us (13%)
  starting transfers between devices  24.2 us (10%)
  local copies, waits for them, and re-layouts  15.8 us (7%)
  between operations  13.2 us (6%)
  other arithmetic  3.46 us (1%)
    reduce_scatter x1, waiting for transfers between devices, per_device(): lax.psum_scatter(contract_first(screened, coeff_full), 'aux', scatter_dim...  43.4 us
    all_gather x1, waiting for transfers between devices, per_device(): dens_full = lax.all_gather(densities, 'aux', axis=0, tiled=True)  39.6 us
    unnamed x4, waiting for transfers between devices  32 us
    ppermute x6, waiting for transfers between devices, from_behind(): return lax.ppermute(array, axis, pairs)  24.8 us
    ppermute x6, starting transfers between devices, from_behind(): return lax.ppermute(array, axis, pairs)  16 us
    dot_general x12, matrix products, product(): jnp.dot(left, right, precision=lax.Precision.HIGHEST, preferred_element_t...  15.3 us
    dot_general x2, matrix products, contract_first(): lax.dot_general(left, right, (((0,), (0,)), ((), ())), precision=lax.Prec...  15.3 us
    ppermute x4, waiting for transfers between devices, collect(): lax.ppermute(going_up, axis, [(d, (d + 1) % ways) for d in range(ways)])  12 us
  transfers between devices with their start and end apart: 16, of which 13 were waited for; matrix products, arithmetic and copies ran while one was open for 8% of the time, Pallas kernels for 0%

profile of v1, /device:TPU:0, one launch (start us, length us, event | category | flops | bytes accessed | tf_op | source)
XLA Modules:
  0.0 239.3 jit_solution(17261781224401961737)
XLA Ops:
  6.5 0.7 all-gather.2.cloned.1.call-update
  7.3 0.7 convert_element_type.3
  8.0 2.3 mul.35
  10.3 4.9 %mul.36 = f32[512,1024]{1,0:T(8,128)} reshape(f32[8,64,16,64]{3,2,1,0:T(8,128)} %mul.35) | data formatting | bytes 4194304 | tf_op jit(solution)/shard_map/mul | solution.py:36
  15.2 2.8 %mul.37 = f32[512,1024]{1,0:T(8,128)S(1)} multiply(f32[512,1024]{1,0:T(8,128)} %param.9, f32[512,1024]{1,0:T(8,128)} %mul.36) | non-fusion elementwise | flops 524288 | bytes 6291456 | tf_op jit(solution)/shard_map/mul | solution.py:36
  18.0 39.6 %all-gather.2.cloned.1.call-done = f32[1024,512]{1,0:T(8,128)} async-done(((f32[256,512]{1,0:T(8,128)}), f32[1024,512]{1,0:T(8,128)}) %all-gather.2.cloned.1.call-update) | async-done | bytes 2097168 | tf_op jit(solution)/shard_map/all_gather | solution.py:56
  57.6 6.1 %convolution_bitcast_fusion = f32[512,512]{0,1:T(8,128)} fusion(f32[512,1024]{1,0:T(8,128)S(1)} %mul.37, f32[1024,512]{1,0:T(8,128)} %all-gather.2.cloned.1.call-done), kind=kOutput, calls=%fused_computation.2 | convolution fusion | flops 3221225472 | bytes 5242880 | tf_op jit(solution)/shard_map/dot_general | solution.py:45
  63.7 2.5 %copy.8 = f32[512,512]{1,0:T(8,128)} copy(f32[512,512]{0,1:T(8,128)} %convolution_bitcast_fusion) | data formatting | bytes 2097152
  66.5 3.1 %convolution_negate_fusion = f32[512,512]{1,0:T(8,128)S(1)} fusion(f32[512,512]{1,0:T(8,128)S(1)} %copy-done, f32[512,512]{1,0:T(8,128)} %param.13), kind=kOutput, calls=%fused_computation.3 | convolution fusion | flops 1610874880 | bytes 3145728 | tf_op jit(solution)/shard_map/dot_general | solution.py:41
  69.9 31.3 %reduce-scatter.7.cloned.1.call-done = f32[64,512]{1,0:T(8,128)} async-done(((f32[512,512]{1,0:T(8,128)}), f32[64,512]{1,0:T(8,128)}) %reduce-scatter.7.cloned.1.call-update) | async-done | bytes 131088
  101.2 2.0 convolution_bitcast_fusion.3
  103.2 23.2 %while.20 = (s32[]{:T(128)}, f32[512,64]{0,1:T(8,128)S(1)}, f32[512,512]{1,0:T(8,128)S(1)}, f32[512,64]{0,1:T(8,128)S(1)}, s32[]{:T(128)}) while((s32[]{:T(128)}, f32[512,64]{0,1:T(8,128)S(1)}, f32[512,512]{1,0:T(8,128)S(1)}, f32[512,64]{0,1:T(8,128)S(1)}, s32[]{:T(128)}) %tuple.34), condition=%wide.region_2.0_spmd, body=%wide.region_1.0_spmd.sunk | while | flops 201359360 | bytes 1966181 | solution.py:68
  103.2 1.1 convolution_add_fusion.5
  104.4 3.4 %collective-permute-start = (f32[512,64]{0,1:T(8,128)S(1)}, f32[512,64]{0,1:T(8,128)S(1)}, u32[]{:S(2)}, u32[]{:S(2)}) collective-permute-start(f32[512,64]{0,1:T(8,128)S(1)} %convolution_add_fusion.5), channel_id=1, source_target_pairs={{0,1},{1,2},{2,3},{4,5},{5,6},{6,7},{8,9},{9,10},{10,11},{12,13},{... | collective-permute-start | bytes 393224 | tf_op jit(solution)/shard_map/while/body/eval_jaxpr/ppermute | solution.py:28
  107.8 2.6 %collective-permute-done = f32[512,64]{0,1:T(8,128)S(1)} collective-permute-done((f32[512,64]{0,1:T(8,128)S(1)}, f32[512,64]{0,1:T(8,128)S(1)}, u32[]{:S(2)}, u32[]{:S(2)}) %collective-permute-start) | collective-permute-done | bytes 131104 | tf_op jit(solution)/shard_map/while/body/eval_jaxpr/ppermute | solution.py:28
  110.4 1.1 convolution_add_fusion.5
  111.5 4.4 %collective-permute-start = (f32[512,64]{0,1:T(8,128)S(1)}, f32[512,64]{0,1:T(8,128)S(1)}, u32[]{:S(2)}, u32[]{:S(2)}) collective-permute-start(f32[512,64]{0,1:T(8,128)S(1)} %convolution_add_fusion.5), channel_id=1, source_target_pairs={{0,1},{1,2},{2,3},{4,5},{5,6},{6,7},{8,9},{9,10},{10,11},{12,13},{... | collective-permute-start | bytes 393224 | tf_op jit(solution)/shard_map/while/body/eval_jaxpr/ppermute | solution.py:28
  115.9 2.5 %collective-permute-done = f32[512,64]{0,1:T(8,128)S(1)} collective-permute-done((f32[512,64]{0,1:T(8,128)S(1)}, f32[512,64]{0,1:T(8,128)S(1)}, u32[]{:S(2)}, u32[]{:S(2)}) %collective-permute-start) | collective-permute-done | bytes 131104 | tf_op jit(solution)/shard_map/while/body/eval_jaxpr/ppermute | solution.py:28
  118.4 1.1 convolution_add_fusion.5
  119.5 4.4 %collective-permute-start = (f32[512,64]{0,1:T(8,128)S(1)}, f32[512,64]{0,1:T(8,128)S(1)}, u32[]{:S(2)}, u32[]{:S(2)}) collective-permute-start(f32[512,64]{0,1:T(8,128)S(1)} %convolution_add_fusion.5), channel_id=1, source_target_pairs={{0,1},{1,2},{2,3},{4,5},{5,6},{6,7},{8,9},{9,10},{10,11},{12,13},{... | collective-permute-start | bytes 393224 | tf_op jit(solution)/shard_map/while/body/eval_jaxpr/ppermute | solution.py:28
  123.9 2.5 %collective-permute-done = f32[512,64]{0,1:T(8,128)S(1)} collective-permute-done((f32[512,64]{0,1:T(8,128)S(1)}, f32[512,64]{0,1:T(8,128)S(1)}, u32[]{:S(2)}, u32[]{:S(2)}) %collective-permute-start) | collective-permute-done | bytes 131104 | tf_op jit(solution)/shard_map/while/body/eval_jaxpr/ppermute | solution.py:28
  126.4 1.1 convolution_add_fusion.2
  127.5 0.8 fusion.1
  128.3 0.8 convolution_bitcast_fusion.2
  129.1 24.6 %while.21 = (s32[]{:T(128)}, f32[512,64]{0,1:T(8,128)S(1)}, f32[512,512]{1,0:T(8,128)S(1)}, f32[512,64]{0,1:T(8,128)S(1)}, s32[]{:T(128)}) while((s32[]{:T(128)}, f32[512,64]{0,1:T(8,128)S(1)}, f32[512,512]{1,0:T(8,128)S(1)}, f32[512,64]{0,1:T(8,128)S(1)}, s32[]{:T(128)}) %tuple.37), condition=%wide.region_4.0_spmd, body=%wide.region_3.0_spmd.sunk | while | flops 201359360 | bytes 1966181 | solution.py:76
  129.1 1.1 convolution_add_fusion.6
  130.2 1.3 collective-permute-start.1
  131.5 6.0 %collective-permute-done.1 = f32[512,64]{0,1:T(8,128)S(1)} collective-permute-done((f32[512,64]{0,1:T(8,128)S(1)}, f32[512,64]{0,1:T(8,128)S(1)}, u32[]{:S(2)}, u32[]{:S(2)}) %collective-permute-start.1) | collective-permute-done | bytes 131104 | tf_op jit(solution)/shard_map/while/body/eval_jaxpr/ppermute | solution.py:28
  137.5 1.1 convolution_add_fusion.6
  138.7 1.3 collective-permute-start.1
  140.0 5.6 %collective-permute-done.1 = f32[512,64]{0,1:T(8,128)S(1)} collective-permute-done((f32[512,64]{0,1:T(8,128)S(1)}, f32[512,64]{0,1:T(8,128)S(1)}, u32[]{:S(2)}, u32[]{:S(2)}) %collective-permute-start.1) | collective-permute-done | bytes 131104 | tf_op jit(solution)/shard_map/while/body/eval_jaxpr/ppermute | solution.py:28
  145.5 1.1 convolution_add_fusion.6
  146.7 1.3 collective-permute-start.1
  148.0 5.7 %collective-permute-done.1 = f32[512,64]{0,1:T(8,128)S(1)} collective-permute-done((f32[512,64]{0,1:T(8,128)S(1)}, f32[512,64]{0,1:T(8,128)S(1)}, u32[]{:S(2)}, u32[]{:S(2)}) %collective-permute-start.1) | collective-permute-done | bytes 131104 | tf_op jit(solution)/shard_map/while/body/eval_jaxpr/ppermute | solution.py:28
  153.8 0.8 constant_dynamic-update-slice_fusion.7
  154.5 1.0 copy-done.4
  155.5 2.6 %collective-permute-start.3 = (f32[512,64]{0,1:T(8,128)S(1)}, f32[512,64]{0,1:T(8,128)S(1)}, u32[]{:S(2)}, u32[]{:S(2)}) collective-permute-start(f32[512,64]{0,1:T(8,128)S(1)} %get-tuple-element.76), channel_id=1, source_target_pairs={{0,28},{4,0},{8,4},{12,8},{16,12},{20,16},{24,20},{28,24},{1,29},{... | collective-permute-start | bytes 393224 | tf_op jit(solution)/shard_map/ppermute | solution.py:18
  158.2 3.2 %collective-permute-done.2 = f32[512,64]{0,1:T(8,128)S(1)} collective-permute-done((f32[512,64]{0,1:T(8,128)S(1)}, f32[512,64]{0,1:T(8,128)S(1)}, u32[]{:S(2)}, u32[]{:S(2)}) %collective-permute-start.2) | collective-permute-done | bytes 131104 | tf_op jit(solution)/shard_map/ppermute | solution.py:15
  161.4 2.6 %collective-permute-start.5 = (f32[512,64]{0,1:T(8,128)S(1)}, f32[512,64]{0,1:T(8,128)S(1)}, u32[]{:S(2)}, u32[]{:S(2)}) collective-permute-start(f32[512,64]{0,1:T(8,128)S(1)} %collective-permute-done.3), channel_id=1, source_target_pairs={{0,28},{4,0},{8,4},{12,8},{16,12},{20,16},{24,20},{28,24},{1,29},{... | collective-permute-start | bytes 393224 | tf_op jit(solution)/shard_map/ppermute | solution.py:18
  165.3 2.5 %collective-permute-done.4 = f32[512,64]{0,1:T(8,128)S(1)} collective-permute-done((f32[512,64]{0,1:T(8,128)S(1)}, f32[512,64]{0,1:T(8,128)S(1)}, u32[]{:S(2)}, u32[]{:S(2)}) %collective-permute-start.4) | collective-permute-done | bytes 131104 | tf_op jit(solution)/shard_map/ppermute | solution.py:15
  167.8 2.6 %collective-permute-start.7 = (f32[512,64]{0,1:T(8,128)S(1)}, f32[512,64]{0,1:T(8,128)S(1)}, u32[]{:S(2)}, u32[]{:S(2)}) collective-permute-start(f32[512,64]{0,1:T(8,128)S(1)} %collective-permute-done.5), channel_id=1, source_target_pairs={{0,28},{4,0},{8,4},{12,8},{16,12},{20,16},{24,20},{28,24},{1,29},{... | collective-permute-start | bytes 393224 | tf_op jit(solution)/shard_map/ppermute | solution.py:18
  170.5 0.7 constant_dynamic-update-slice_fusion.4
  171.1 0.7 constant_dynamic-update-slice_fusion.3
  171.8 2.3 collective-permute-done.6
  174.2 0.7 constant_dynamic-update-slice_fusion.2
  175.5 4.0 %collective-permute-done.8 = f32[512,64]{0,1:T(8,128)S(1)} collective-permute-done((f32[512,64]{0,1:T(8,128)S(1)}, f32[512,64]{0,1:T(8,128)S(1)}, u32[]{:S(2)}, u32[]{:S(2)}) %collective-permute-start.8) | collective-permute-done | bytes 131104 | tf_op jit(solution)/shard_map/ppermute | solution.py:15
  180.1 9.2 %fusion.2 = f32[1024,512]{1,0:T(8,128)} fusion(f32[512,1024]{1,0:T(8,128)S(1)} %copy-done.2, f32[512,512]{0,1:T(8,128)} %constant_dynamic-update-slice_fusion), kind=kOutput, calls=%fused_computation.18 | convolution fusion | flops 3221225472 | bytes 5242880 | tf_op jit(solution)/shard_map/dot_general | solution.py:45
  189.4 43.4 %reduce-scatter.5.cloned.1.call-done = f32[256,512]{1,0:T(8,128)} async-done(((f32[1024,512]{1,0:T(8,128)}), f32[256,512]{1,0:T(8,128)}) %reduce-scatter.5.cloned.1.call-update) | async-done | bytes 524304 | tf_op jit(solution)/shard_map/reduce_scatter | solution.py:79
  (29 shorter events, 3.4 us)
Async XLA Ops:
  6.5 60.0 %copy-start = (f32[512,512]{1,0:T(8,128)S(1)}, f32[512,512]{1,0:T(8,128)}, u32[]{:S(2)}) copy-start(f32[512,512]{1,0:T(8,128)} %param.12) | copy-start | bytes 3145732
  6.5 51.1 %all-gather.2.cloned.1.call-start = ((), (), s32[]{:S(2)}) async-start(), calls=%async_computation.2 | async-start | bytes 2621440 | tf_op jit(solution)/shard_map/all_gather | solution.py:56
  7.3 93.9 %reduce-scatter.7.cloned.1.call-start = ((), (), s32[]{:S(2)}) async-start(), calls=%async_computation.4 | async-start | bytes 1179648
  18.0 45.7 %copy-start.1 = (f32[512,1024]{1,0:T(8,128)}, f32[512,1024]{1,0:T(8,128)S(1)}, u32[]{:S(2)}) copy-start(f32[512,1024]{1,0:T(8,128)S(1)} %mul.37) | copy-start | bytes 6291460
  66.3 166.5 %reduce-scatter.5.cloned.1.call-start = ((), (), s32[]{:S(2)}) async-start(), calls=%async_computation.3 | async-start | bytes 2621440 | tf_op jit(solution)/shard_map/reduce_scatter | solution.py:79
  104.4 6.0 %collective-permute-start = (f32[512,64]{0,1:T(8,128)S(1)}, f32[512,64]{0,1:T(8,128)S(1)}, u32[]{:S(2)}, u32[]{:S(2)}) collective-permute-start(f32[512,64]{0,1:T(8,128)S(1)} %convolution_add_fusion.5), channel_id=1, source_target_pairs={{0,1},{1,2},{2,3},{4,5},{5,6},{6,7},{8,9},{9,10},{10,11},{12,13},{... | collective-permute-start | bytes 393224 | tf_op jit(solution)/shard_map/while/body/eval_jaxpr/ppermute | solution.py:28
  111.5 6.9 %collective-permute-start = (f32[512,64]{0,1:T(8,128)S(1)}, f32[512,64]{0,1:T(8,128)S(1)}, u32[]{:S(2)}, u32[]{:S(2)}) collective-permute-start(f32[512,64]{0,1:T(8,128)S(1)} %convolution_add_fusion.5), channel_id=1, source_target_pairs={{0,1},{1,2},{2,3},{4,5},{5,6},{6,7},{8,9},{9,10},{10,11},{12,13},{... | collective-permute-start | bytes 393224 | tf_op jit(solution)/shard_map/while/body/eval_jaxpr/ppermute | solution.py:28
  119.5 6.9 %collective-permute-start = (f32[512,64]{0,1:T(8,128)S(1)}, f32[512,64]{0,1:T(8,128)S(1)}, u32[]{:S(2)}, u32[]{:S(2)}) collective-permute-start(f32[512,64]{0,1:T(8,128)S(1)} %convolution_add_fusion.5), channel_id=1, source_target_pairs={{0,1},{1,2},{2,3},{4,5},{5,6},{6,7},{8,9},{9,10},{10,11},{12,13},{... | collective-permute-start | bytes 393224 | tf_op jit(solution)/shard_map/while/body/eval_jaxpr/ppermute | solution.py:28
  126.4 1.9 copy-start.3
  130.2 7.3 %collective-permute-start.1 = (f32[512,64]{0,1:T(8,128)S(1)}, f32[512,64]{0,1:T(8,128)S(1)}, u32[]{:S(2)}, u32[]{:S(2)}) collective-permute-start(f32[512,64]{0,1:T(8,128)S(1)} %convolution_add_fusion.6), channel_id=1, source_target_pairs={{1,0},{2,1},{3,2},{5,4},{6,5},{7,6},{9,8},{10,9},{11,10},{13,12},{... | collective-permute-start | bytes 393224 | tf_op jit(solution)/shard_map/while/body/eval_jaxpr/ppermute | solution.py:28
  138.7 6.9 %collective-permute-start.1 = (f32[512,64]{0,1:T(8,128)S(1)}, f32[512,64]{0,1:T(8,128)S(1)}, u32[]{:S(2)}, u32[]{:S(2)}) collective-permute-start(f32[512,64]{0,1:T(8,128)S(1)} %convolution_add_fusion.6), channel_id=1, source_target_pairs={{1,0},{2,1},{3,2},{5,4},{6,5},{7,6},{9,8},{10,9},{11,10},{13,12},{... | collective-permute-start | bytes 393224 | tf_op jit(solution)/shard_map/while/body/eval_jaxpr/ppermute | solution.py:28
  146.7 7.0 %collective-permute-start.1 = (f32[512,64]{0,1:T(8,128)S(1)}, f32[512,64]{0,1:T(8,128)S(1)}, u32[]{:S(2)}, u32[]{:S(2)}) collective-permute-start(f32[512,64]{0,1:T(8,128)S(1)} %convolution_add_fusion.6), channel_id=1, source_target_pairs={{1,0},{2,1},{3,2},{5,4},{6,5},{7,6},{9,8},{10,9},{11,10},{13,12},{... | collective-permute-start | bytes 393224 | tf_op jit(solution)/shard_map/while/body/eval_jaxpr/ppermute | solution.py:28
  153.6 26.5 %copy-start.2 = (f32[512,1024]{1,0:T(8,128)S(1)}, f32[512,1024]{1,0:T(8,128)}, u32[]{:S(2)}) copy-start(f32[512,1024]{1,0:T(8,128)} %copy-done.1) | copy-start | bytes 6291460
  154.5 1.0 copy-start.4
  155.5 5.9 %collective-permute-start.2 = (f32[512,64]{0,1:T(8,128)S(1)}, f32[512,64]{0,1:T(8,128)S(1)}, u32[]{:S(2)}, u32[]{:S(2)}) collective-permute-start(f32[512,64]{0,1:T(8,128)S(1)} %get-tuple-element.76), channel_id=1, source_target_pairs={{0,4},{4,8},{8,12},{12,16},{16,20},{20,24},{24,28},{28,0},{1,5},{5... | collective-permute-start | bytes 393224 | tf_op jit(solution)/shard_map/ppermute | solution.py:15
  155.5 5.9 %collective-permute-start.3 = (f32[512,64]{0,1:T(8,128)S(1)}, f32[512,64]{0,1:T(8,128)S(1)}, u32[]{:S(2)}, u32[]{:S(2)}) collective-permute-start(f32[512,64]{0,1:T(8,128)S(1)} %get-tuple-element.76), channel_id=1, source_target_pairs={{0,28},{4,0},{8,4},{12,8},{16,12},{20,16},{24,20},{28,24},{1,29},{... | collective-permute-start | bytes 393224 | tf_op jit(solution)/shard_map/ppermute | solution.py:18
  161.4 6.5 %collective-permute-start.4 = (f32[512,64]{0,1:T(8,128)S(1)}, f32[512,64]{0,1:T(8,128)S(1)}, u32[]{:S(2)}, u32[]{:S(2)}) collective-permute-start(f32[512,64]{0,1:T(8,128)S(1)} %collective-permute-done.2), channel_id=1, source_target_pairs={{0,4},{4,8},{8,12},{12,16},{16,20},{20,24},{24,28},{28,0},{1,5},{5... | collective-permute-start | bytes 393224 | tf_op jit(solution)/shard_map/ppermute | solution.py:15
  161.4 6.5 %collective-permute-start.5 = (f32[512,64]{0,1:T(8,128)S(1)}, f32[512,64]{0,1:T(8,128)S(1)}, u32[]{:S(2)}, u32[]{:S(2)}) collective-permute-start(f32[512,64]{0,1:T(8,128)S(1)} %collective-permute-done.3), channel_id=1, source_target_pairs={{0,28},{4,0},{8,4},{12,8},{16,12},{20,16},{24,20},{28,24},{1,29},{... | collective-permute-start | bytes 393224 | tf_op jit(solution)/shard_map/ppermute | solution.py:18
  167.8 6.3 %collective-permute-start.6 = (f32[512,64]{0,1:T(8,128)S(1)}, f32[512,64]{0,1:T(8,128)S(1)}, u32[]{:S(2)}, u32[]{:S(2)}) collective-permute-start(f32[512,64]{0,1:T(8,128)S(1)} %collective-permute-done.4), channel_id=1, source_target_pairs={{0,4},{4,8},{8,12},{12,16},{16,20},{20,24},{24,28},{28,0},{1,5},{5... | collective-permute-start | bytes 393224 | tf_op jit(solution)/shard_map/ppermute | solution.py:15
  167.8 7.0 %collective-permute-start.7 = (f32[512,64]{0,1:T(8,128)S(1)}, f32[512,64]{0,1:T(8,128)S(1)}, u32[]{:S(2)}, u32[]{:S(2)}) collective-permute-start(f32[512,64]{0,1:T(8,128)S(1)} %collective-permute-done.5), channel_id=1, source_target_pairs={{0,28},{4,0},{8,4},{12,8},{16,12},{20,16},{24,20},{28,24},{1,29},{... | collective-permute-start | bytes 393224 | tf_op jit(solution)/shard_map/ppermute | solution.py:18
  174.2 5.3 %collective-permute-start.8 = (f32[512,64]{0,1:T(8,128)S(1)}, f32[512,64]{0,1:T(8,128)S(1)}, u32[]{:S(2)}, u32[]{:S(2)}) collective-permute-start(f32[512,64]{0,1:T(8,128)S(1)} %collective-permute-done.6), channel_id=1, source_target_pairs={{0,4},{4,8},{8,12},{12,16},{16,20},{20,24},{24,28},{28,0},{1,5},{5... | collective-permute-start | bytes 393224 | tf_op jit(solution)/shard_map/ppermute | solution.py:15
Sparse Core Ops, SparseCore 0:
  8.9 48.6 all-gather.1
  66.4 34.7 reduce-scatter.6
  189.5 43.2 reduce-scatter.4
